TPU v7x, 512 devices: a whole 4x8x8 slice. The times are simulated.
512 devices in a mesh: ctx: 16 (over z_hi, x), tp: 8 (over y), dp: 4 (over z_lo, core).
Axes of the slice: x: 4, y: 8, z: 8 (z_hi: 4, z_lo: 2; z = z_hi * 2 + z_lo), core: 2. Of those that a mesh axis runs over, the one named last changes fastest.
Arguments:
- q_raw: bfloat16 [4, 2048, 2048], P('dp', 'ctx', 'tp'), may hold values from -60 to 60
- k_raw: bfloat16 [4, 2048, 2048], P('dp', 'ctx', 'tp'), may hold values from -60 to 60
- value: bfloat16 [4, 2048, 2048], P('dp', 'ctx', 'tp'), may hold values from -6 to 6
- d_out: bfloat16 [4, 2048, 2048], P('dp', 'ctx', 'tp'), may hold values from -6 to 6
- q_gain: float32 [128], replicated, may hold values from 1.3 to 5
- k_gain: float32 [128], replicated, may hold values from 1.3 to 5
Outputs:
- q_raw_grad: bfloat16 [4, 2048, 2048], P('dp', 'ctx', 'tp')
- k_raw_grad: bfloat16 [4, 2048, 2048], P('dp', 'ctx', 'tp')
- value_grad: bfloat16 [4, 2048, 2048], P('dp', 'ctx', 'tp')
- q_gain_grad: float32 [128], replicated
- k_gain_grad: float32 [128], replicated
All inputs are finite; a program needn't handle non-finite values.
Results may differ from a plain program's by a relative error of at most 0.028.
The roundings to bfloat16 on the way count: a program that leaves them out, or rounds other values in their place, can miss the bound.
Values may be sent and summed in bfloat16 or wider, within the bound.
A program may use at most 64 MiB of HBM per device.

v0:
```python
import math

import jax
import jax.numpy as jnp
from jax import lax
from jax.sharding import PartitionSpec as P

EPSILON = 1e-06


def normalize(raw, gain, heads_here):
    rows = raw.shape[0]
    width = gain.shape[0]
    values = raw.astype(jnp.float32).reshape(rows, heads_here, width)
    inverse = lax.rsqrt(jnp.mean(values * values, axis=2, keepdims=True) + EPSILON)
    unit = values * inverse
    return (unit, inverse, (unit * gain).astype(jnp.bfloat16))


def restore(grad_normed, unit, inverse, gain):
    scaled = grad_normed * gain
    back = inverse * (scaled - unit * jnp.mean(scaled * unit, axis=2, keepdims=True))
    return (back, jnp.sum(grad_normed * unit, axis=(0, 1)))


def block_weights(query_normed, query_out, log_total, delta, key_normed, key_value_pair, scale):
    scores = (
        jnp.einsum("qhd,khd->hqk", query_normed, key_normed, preferred_element_type=jnp.float32)
        * scale
    )
    prob = jnp.exp(scores - log_total[:, :, None])
    dprob = jnp.einsum(
        "qhd,khd->hqk", query_out, key_value_pair, preferred_element_type=jnp.float32
    )
    prob_low = prob.astype(jnp.bfloat16)
    dscore = (prob * (dprob - delta[:, :, None]) * scale).astype(jnp.bfloat16)
    return (prob_low, dscore)


def key_block_terms(query_normed, query_out, log_total, delta, key_normed, key_value_pair, scale):
    prob_low, dscore = block_weights(
        query_normed, query_out, log_total, delta, key_normed, key_value_pair, scale
    )
    dkey = jnp.einsum("hqk,qhd->khd", dscore, query_normed, preferred_element_type=jnp.float32)
    dval = jnp.einsum("hqk,qhd->khd", prob_low, query_out, preferred_element_type=jnp.float32)
    return (dkey, dval)


def local(q_raw, k_raw, value, d_out, q_gain, k_gain):
    width = q_gain.shape[0]
    rows = q_raw.shape[1]
    heads_here = q_raw.shape[2] // width
    flat = heads_here * width
    scale = width ** (-0.5)
    q_unit, q_inverse, q_normed = normalize(q_raw[0], q_gain, heads_here)
    k_unit, k_inverse, k_normed = normalize(k_raw[0], k_gain, heads_here)
    own_value = value[0]
    own_out_flat = d_out[0]
    own_out = own_out_flat.reshape(rows, heads_here, width)
    all_keys, all_values = (
        lax.all_gather(k_normed.reshape(rows, flat), "ctx", axis=0, tiled=True),
        lax.all_gather(own_value, "ctx", axis=0, tiled=True),
    )
    length = all_keys.shape[0]
    block = min(512, length)
    block_count = length // block

    def key_slice(begin, size):
        keys = lax.dynamic_slice_in_dim(all_keys, begin, size, 0).reshape(size, heads_here, width)
        vals = lax.dynamic_slice_in_dim(all_values, begin, size, 0).reshape(size, heads_here, width)
        return (keys, vals)

    def statistics(index, carry):
        top, total, weighted = carry
        keys, vals = key_slice(index * block, block)
        scores = (
            jnp.einsum("qhd,khd->hqk", q_normed, keys, preferred_element_type=jnp.float32) * scale
        )
        dprob = jnp.einsum("qhd,khd->hqk", own_out, vals, preferred_element_type=jnp.float32)
        new_top = jnp.maximum(top, jnp.max(scores, axis=2))
        factor = jnp.exp(top - new_top)
        expo = jnp.exp(scores - new_top[:, :, None])
        return (
            new_top,
            total * factor + jnp.sum(expo, axis=2),
            weighted * factor + jnp.sum(expo * dprob, axis=2),
        )

    start_top = jnp.full((heads_here, rows), -jnp.inf, jnp.float32)
    zero_stat = jnp.zeros((heads_here, rows), jnp.float32)
    top, total, weighted = lax.fori_loop(
        0, block_count, statistics, (start_top, zero_stat, zero_stat)
    )
    log_total = top + jnp.log(total)
    delta = weighted / total

    def query_pass(index, acc):
        keys, vals = key_slice(index * block, block)
        prob_low, dscore = block_weights(q_normed, own_out, log_total, delta, keys, vals, scale)
        return acc + jnp.einsum("hqk,khd->qhd", dscore, keys, preferred_element_type=jnp.float32)

    dq_normed = lax.fori_loop(
        0, block_count, query_pass, jnp.zeros((rows, heads_here, width), jnp.float32)
    )
    dq_back, q_gain_part = restore(dq_normed, q_unit, q_inverse, q_gain)
    size = math.gcd(lax.axis_size("ctx") * rows, 512)

    def one_block(index):
        keys, vals = key_slice(index * size, size)
        dkey, dval = key_block_terms(q_normed, own_out, log_total, delta, keys, vals, scale)
        return jnp.concatenate([dkey.reshape(size, flat), dval.reshape(size, flat)], axis=1)

    summed = lax.psum_scatter(
        lax.map(one_block, jnp.arange(lax.axis_size("ctx") * rows // size))
        .reshape(lax.axis_size("ctx") * rows, 2 * flat)
        .astype(jnp.bfloat16),
        "ctx",
        scatter_dimension=0,
        tiled=True,
    ).astype(jnp.float32)
    dk_normed = summed[:, :flat]
    dv_sum = summed[:, flat:]
    dk_back, k_gain_part = restore(
        dk_normed.reshape(rows, heads_here, width), k_unit, k_inverse, k_gain
    )
    q_gain_total, k_gain_total = lax.psum((q_gain_part, k_gain_part), ("ctx", "tp", "dp"))
    q_grad = dq_back.reshape(rows, flat).astype(jnp.bfloat16)[None]
    k_grad = dk_back.reshape(rows, flat).astype(jnp.bfloat16)[None]
    value_grad = dv_sum.astype(jnp.bfloat16)[None]
    return (q_grad, k_grad, value_grad, q_gain_total / length, k_gain_total / length)


def solution(mesh):
    return jax.shard_map(
        local,
        mesh=mesh,
        in_specs=(
            P("dp", "ctx", "tp"),
            P("dp", "ctx", "tp"),
            P("dp", "ctx", "tp"),
            P("dp", "ctx", "tp"),
            P(),
            P(),
        ),
        out_specs=(P("dp", "ctx", "tp"), P("dp", "ctx", "tp"), P("dp", "ctx", "tp"), P(), P()),
        check_vma=False,
    )
```

profile of v0, /device:TPU:1, one launch (start us, length us, event | category | flops | bytes accessed | tf_op | source)
XLA Modules:
  0.0 363.0 jit_solution(17884126247453620999)
XLA Ops:
  7.9 0.9 reshape.126
  9.2 1.5 multiply_convert_fusion.2
  10.8 1.6 copy.113
  12.5 1.0 copy.114
  13.6 0.9 copy.110
  15.4 59.9 %all-gather.4.cloned.1.call-done = bf16[2048,256]{1,0:T(8,128)(2,1)} async-done(((bf16[128,256]{1,0:T(8,128)(2,1)}), bf16[2048,256]{1,0:T(8,128)(2,1)}) %all-gather.4.cloned.1.call-update) | async-done | bytes 1048592 | tf_op jit(solution)/shard_map/all_gather | solution.py:61
  75.4 1.5 copy.118
  76.9 60.4 %all-gather.6.cloned.1.call-done = bf16[1,2048,256]{1,2,0:T(8,128)(2,1)} async-done(((bf16[1,128,256]{1,2,0:T(8,128)(2,1)}), bf16[1,2048,256]{1,2,0:T(8,128)(2,1)}) %all-gather.6.cloned.1.call-update) | async-done | bytes 1048592 | tf_op jit(solution)/shard_map/all_gather | solution.py:62
  137.3 7.0 %while.43 = (s32[]{:T(128)}, f32[2,128]{1,0:T(2,128)S(1)}, f32[2,128]{1,0:T(2,128)S(1)}, f32[2,128]{1,0:T(2,128)S(1)}, bf16[2048,256]{0,1:T(8,128)(2,1)S(1)}, /*...) while((s32[]{:T(128)}, f32[2,128]{1,0:T(2,128)S(1)}, ...), condition=%wide.region_6.0_spmd.clone, body=%wide.region_2.0_spmd.clone.sunk | while | flops 68028160 | bytes 3295418 | solution.py:91
  137.3 1.0 constant_dynamic-slice_fusion.10
  139.0 1.0 constant_dynamic-slice_fusion.10
  140.8 1.0 constant_dynamic-slice_fusion.10
  142.6 1.0 constant_dynamic-slice_fusion.10
  144.3 16.4 %while.42 = (s32[]{:T(128)}, bf16[4,512,512]{1,2,0:T(8,128)(2,1)}, s32[4]{0:T(128)S(1)}, bf16[2048,256]{0,1:T(8,128)(2,1)S(1)}, bf16[128,2,128]{0,2,1:T(8,128)(2...) while((s32[]{:T(128)}, bf16[4,512,512]{1,2,0:T(8,128)(2,1)}, ...), condition=%wide.region_11.12_spmd, body=%wide.region_10.0_spmd.sunk | while | flops 136183808 | bytes 4982983 | solution.py:114
  145.6 1.0 constant_dynamic-slice_fusion.9
  147.6 0.8 fusion.88
  149.7 1.0 constant_dynamic-slice_fusion.9
  151.7 0.9 fusion.88
  153.8 1.0 constant_dynamic-slice_fusion.9
  155.8 0.8 fusion.88
  157.9 1.0 constant_dynamic-slice_fusion.9
  159.9 0.9 fusion.88
  160.8 4.1 %copy.123 = bf16[4,512,512]{2,1,0:T(8,128)(2,1)} copy(bf16[4,512,512]{1,2,0:T(8,128)(2,1)} %get-tuple-element.336) | data formatting | bytes 4194304 | tf_op jit(solution)/shard_map/convert_element_type | solution.py:116
  165.0 7.3 %while.44 = (s32[]{:T(128)}, f32[128,2,128]{0,2,1:T(8,128)S(1)}, bf16[2048,256]{0,1:T(8,128)(2,1)S(1)}, bf16[128,2,128]{2,0,1:T(8,128)(2,1)S(1)}, f32[2,128]{1,0...) while((s32[]{:T(128)}, f32[128,2,128]{0,2,1:T(8,128)S(1)}, ...), condition=%wide.region_8.0_spmd.clone, body=%wide.region_7.0_spmd.clone.sunk | while | flops 101515264 | bytes 3279033 | solution.py:102
  165.0 1.0 constant_dynamic-slice_fusion.11
  166.8 1.0 constant_dynamic-slice_fusion.11
  168.7 1.0 constant_dynamic-slice_fusion.11
  170.5 1.0 constant_dynamic-slice_fusion.11
  173.3 82.7 %reduce-scatter.2.cloned.1.call-done = bf16[128,512]{1,0:T(8,128)(2,1)} async-done(((bf16[2048,512]{1,0:T(8,128)(2,1)}), bf16[128,512]{1,0:T(8,128)(2,1)}) %reduce-scatter.2.cloned.1.call-update) | async-done | bytes 131088 | tf_op jit(solution)/shard_map/reduce_scatter | solution.py:113
  255.9 1.5 slice_bitcast_fusion
  258.1 1.5 multiply_reduce_fusion
  259.7 96.3 %all-reduce = (f32[128]{0:T(128)S(1)}, f32[128]{0:T(128)S(1)}) all-reduce(f32[128]{0:T(128)S(1)} %get-tuple-element.541, f32[128]{0:T(128)S(1)} %bitcast_reduce_fusion), channel_id=1, replica_groups=mesh['ctx'=16,'tp'=8,'dp'=4] {'ctx','tp','dp'}, use_global_device_ids=true, to_apply=%region_15.16 | all-reduce | flops 256 | bytes 2048 | tf_op jit(solution)/shard_map/psum | solution.py:126
  (86 shorter events, 16.7 us)
Async XLA Ops:
  7.2 68.2 %all-gather.4.cloned.1.call-start = ((), (), s32[]{:S(2)}) async-start(), calls=%async_computation.1 | async-start | bytes 1114112 | tf_op jit(solution)/shard_map/all_gather | solution.py:61
  10.7 126.5 %all-gather.6.cloned.1.call-start = ((), (), s32[]{:S(2)}) async-start(), calls=%async_computation.3 | async-start | bytes 1114112 | tf_op jit(solution)/shard_map/all_gather | solution.py:62
  12.4 243.6 %reduce-scatter.2.cloned.1.call-start = ((), (), s32[]{:S(2)}) async-start(), calls=%async_computation.2 | async-start | bytes 2228224 | tf_op jit(solution)/shard_map/reduce_scatter | solution.py:113
  164.9 7.3 %copy-start.1 = (f32[128]{0:T(128)S(1)}, f32[128]{0:T(128)}, u32[]{:S(2)}) copy-start(f32[128]{0:T(128)} %param.16) | copy-start | bytes 1540
  165.0 92.6 %copy-start.2 = (f32[128]{0:T(128)S(1)}, f32[128]{0:T(128)}, u32[]{:S(2)}) copy-start(f32[128]{0:T(128)} %param.17) | copy-start | bytes 1540
  165.0 93.2 %copy-start = (bf16[1,128,256]{2,1,0:T(8,128)(2,1)S(1)}, bf16[1,128,256]{2,1,0:T(8,128)(2,1)}, u32[]{:S(2)}) copy-start(bf16[1,128,256]{2,1,0:T(8,128)(2,1)} %param.13) | copy-start | bytes 196612
Sparse Core Ops, SparseCore 0:
  11.6 63.7 all-gather.3
  78.9 58.3 all-gather.5
  165.1 90.8 reduce-scatter.1
where the time goes:
time: 364 us; the launch traced here: 363 us
  waiting for transfers between devices  203 us (56%)
  blocking collectives  96.3 us (26%)
  local copies, waits for them, and re-layouts  26.5 us (7%)
  between operations  14 us (4%)
  other arithmetic  10.5 us (3%)
  matrix products  9.47 us (3%)
    psum x1, blocking collectives, local(): lax.psum((q_gain_part, k_gain_part), ('ctx', 'tp', 'dp'))  96.3 us
    reduce_scatter x1, waiting for transfers between devices, local(): lax.psum_scatter(lax.map(one_block, jnp.arange(lax.axis_size('ctx') * row...  82.7 us
    all_gather x1, waiting for transfers between devices, local(): lax.all_gather(own_value, 'ctx', axis=0, tiled=True)  60.4 us
    all_gather x1, waiting for transfers between devices, local(): lax.all_gather(k_normed.reshape(rows, flat), 'ctx', axis=0, tiled=True)  59.9 us
    dynamic_slice x12, local copies, waits for them, and re-layouts, key_slice(): lax.dynamic_slice_in_dim(all_values, begin, size, 0)  12 us
  transfers between devices with their start and end apart: 3, of which 3 were waited for; matrix products, arithmetic and copies ran while one was open for 4% of the time, Pallas kernels for 0%

commit v1 on v0

v1 whole, which is shorter than its diff:
```python
import functools

import jax
import jax.numpy as jnp
from jax import lax
from jax.experimental import pallas as pl
from jax.experimental.pallas import tpu as pltpu
from jax.sharding import PartitionSpec as P

EPSILON = 1e-06
SIDE = 4
MESH = pl.DeviceIdType.MESH


def kernel(
    sizes,
    q_ref,
    k_ref,
    v_ref,
    o_ref,
    q_gain_ref,
    k_gain_ref,
    dq_out,
    dk_out,
    dv_out,
    gain_out,
    q_raw,
    k_raw,
    v_all,
    o_all,
    q_normed,
    q_unit,
    q_inverse,
    k_normed,
    k_unit,
    k_inverse,
    k_turned,
    expo,
    dprob,
    stat_own,
    stat_in,
    acc,
    dkv_send,
    dkv_in,
    dq_own,
    dq_send,
    dq_in,
    gain_dp,
    gain_x,
    gain_z,
    gain_tp,
    send_sem,
    recv_sem,
):
    n_tp, n_dp, heads, length = sizes
    rows = q_ref.shape[0]
    width = q_gain_ref.shape[1]
    keys = SIDE * rows
    flat = heads * width
    scale = width ** (-0.5)
    ctx = lax.axis_index("ctx")
    tp = lax.axis_index("tp")
    dp = lax.axis_index("dp")
    x = lax.rem(ctx, SIDE)
    z = ctx // SIDE

    def along_x(step):
        return {"ctx": z * SIDE + lax.rem(x + step, SIDE), "tp": tp, "dp": dp}

    def along_z(step):
        return {"ctx": lax.rem(z + step, SIDE) * SIDE + x, "tp": tp, "dp": dp}

    def along_dp(step):
        return {"ctx": ctx, "tp": tp, "dp": lax.rem(dp + step, n_dp)}

    def along_tp(step):
        return {"ctx": ctx, "tp": lax.rem(tp + step, n_tp), "dp": dp}

    count = [0]
    started = []

    def copy(src, dst, device):
        index = count[0]
        count[0] += 1
        one = pltpu.make_async_remote_copy(
            src_ref=src,
            dst_ref=dst,
            send_sem=send_sem.at[index],
            recv_sem=recv_sem.at[index],
            device_id=device,
            device_id_type=MESH,
        )
        started.append(one)
        return one

    def cols(head):
        return slice(head * width, (head + 1) * width)

    barrier = pltpu.get_barrier_semaphore()
    partners = (
        [along_x(step) for step in range(1, SIDE)]
        + [along_z(step) for step in range(1, SIDE)]
        + [along_dp(step) for step in range(1, n_dp)]
        + [along_tp(step) for step in range(1, n_tp)]
    )
    for partner in partners:
        pl.semaphore_signal(barrier, inc=1, device_id=partner, device_id_type=MESH)
    pl.semaphore_wait(barrier, len(partners))

    q_up = copy(q_ref, q_raw.at[1], along_z(1))
    q_down = copy(q_ref, q_raw.at[3], along_z(3))
    o_up = copy(o_ref, o_all.at[1], along_z(1))
    o_down = copy(o_ref, o_all.at[3], along_z(3))
    k_up = copy(k_ref, k_raw.at[1], along_x(1))
    k_down = copy(k_ref, k_raw.at[3], along_x(3))
    v_up = copy(v_ref, v_all.at[1], along_x(1))
    v_down = copy(v_ref, v_all.at[3], along_x(3))
    for one in (q_up, o_down, o_up, q_down, k_up, v_down, v_up, k_down):
        one.start()
    q_far = copy(q_raw.at[1], q_raw.at[2], along_z(1))
    o_far = copy(o_all.at[3], o_all.at[2], along_z(3))
    k_far = copy(k_raw.at[1], k_raw.at[2], along_x(1))
    v_far = copy(v_all.at[3], v_all.at[2], along_x(3))

    v_all[0] = v_ref[...]
    o_all[0] = o_ref[...]
    acc[...] = jnp.zeros_like(acc)
    stat_own[...] = jnp.zeros_like(stat_own)

    def norm_q(slot, raw):
        for head in range(heads):
            values = raw[:, cols(head)].astype(jnp.float32)
            inverse = lax.rsqrt(jnp.mean(values * values, axis=1, keepdims=True) + EPSILON)
            unit = values * inverse
            q_unit[slot, :, cols(head)] = unit
            q_normed[slot, :, cols(head)] = (unit * q_gain_ref[...]).astype(jnp.bfloat16)
            if slot == 0:
                q_inverse[:, cols(head)] = jnp.broadcast_to(inverse, (rows, width))

    def norm_k(slot, raw):
        here = slice(slot * rows, (slot + 1) * rows)
        for head in range(heads):
            values = raw[:, cols(head)].astype(jnp.float32)
            inverse = lax.rsqrt(jnp.mean(values * values, axis=1, keepdims=True) + EPSILON)
            unit = values * inverse
            normed = unit * k_gain_ref[...]
            k_unit[here, cols(head)] = unit
            k_normed[here, cols(head)] = normed.astype(jnp.bfloat16)
            k_turned[head, :, here] = normed.astype(jnp.bfloat16).T
            if slot == 0:
                k_inverse[:, cols(head)] = jnp.broadcast_to(inverse, (rows, width))

    norm_q(0, q_ref[...])
    norm_k(0, k_ref[...])

    k_up.wait_recv()
    k_far.start()
    v_down.wait_recv()
    v_far.start()
    norm_k(1, k_raw[1])
    k_down.wait_recv()
    norm_k(3, k_raw[3])
    q_up.wait_recv()
    q_far.start()
    o_down.wait_recv()
    o_far.start()
    k_far.wait_recv()
    norm_k(2, k_raw[2])
    v_up.wait_recv()
    v_far.wait_recv()

    def contract_last(left, right):
        return lax.dot_general(
            left, right, (((1,), (1,)), ((), ())), preferred_element_type=jnp.float32
        )

    stat_copies = {}

    def first_pass(slot):
        for head in range(heads):
            scores = (
                contract_last(k_normed[:, cols(head)], q_normed[slot, :, cols(head)]) * scale
            )
            top = jnp.max(scores, axis=0, keepdims=True)
            weights = jnp.exp(scores - top)
            slopes = contract_last(
                v_all[:, :, cols(head)].reshape(keys, width), o_all[slot, :, cols(head)]
            )
            expo[slot, head] = weights
            dprob[slot, head] = slopes
            stat_own[slot, 3 * head : 3 * head + 1] = top
            stat_own[slot, 3 * head + 1 : 3 * head + 2] = jnp.sum(weights, axis=0, keepdims=True)
            stat_own[slot, 3 * head + 2 : 3 * head + 3] = jnp.sum(
                weights * slopes, axis=0, keepdims=True
            )
        for step in range(1, SIDE):
            there = (slot + step) % SIDE
            one = copy(stat_own.at[slot], stat_in.at[there, step], along_z(step))
            stat_copies[there, step] = one
            one.start()

    first_pass(0)
    o_up.wait_recv()
    norm_q(1, q_raw[1])
    first_pass(1)
    q_down.wait_recv()
    norm_q(3, q_raw[3])
    first_pass(3)
    q_far.wait_recv()
    norm_q(2, q_raw[2])
    o_far.wait_recv()
    first_pass(2)

    dq_copies = []
    q_gain_part = jnp.zeros((1, width), jnp.float32)

    def second_pass(slot):
        for step in range(1, SIDE):
            stat_copies[slot, step].wait_recv()
        part = jnp.zeros((1, width), jnp.float32)
        for head in range(heads):
            tops = [stat_own[slot, 3 * head : 3 * head + 1]]
            totals = [stat_own[slot, 3 * head + 1 : 3 * head + 2]]
            weighted = [stat_own[slot, 3 * head + 2 : 3 * head + 3]]
            for step in range(1, SIDE):
                tops.append(stat_in[slot, step, 3 * head : 3 * head + 1])
                totals.append(stat_in[slot, step, 3 * head + 1 : 3 * head + 2])
                weighted.append(stat_in[slot, step, 3 * head + 2 : 3 * head + 3])
            top = functools.reduce(jnp.maximum, tops)
            factors = [jnp.exp(one - top) for one in tops]
            total = sum(one * factor for one, factor in zip(totals, factors))
            delta = sum(one * factor for one, factor in zip(weighted, factors)) / total
            prob = expo[slot, head] * (factors[0] / total)
            dscore = (prob * (dprob[slot, head] - delta) * scale).astype(jnp.bfloat16)
            prob_low = prob.astype(jnp.bfloat16)
            turned = jnp.dot(k_turned[head], dscore, preferred_element_type=jnp.float32)
            dq = turned.T
            part += jnp.sum(dq * q_unit[slot, :, cols(head)], axis=0, keepdims=True)
            if slot == 0:
                dq_own[:, cols(head)] = dq
            else:
                dq_send[slot, :, cols(head)] = dq.astype(jnp.bfloat16)
            acc[:, cols(head)] += jnp.dot(
                dscore, q_normed[slot, :, cols(head)], preferred_element_type=jnp.float32
            )
            acc[:, flat + head * width : flat + (head + 1) * width] += jnp.dot(
                prob_low, o_all[slot, :, cols(head)], preferred_element_type=jnp.float32
            )
        if slot > 0:
            one = copy(dq_send.at[slot], dq_in.at[slot], along_z(SIDE - slot))
            dq_copies.append(one)
            one.start()
        return part

    for slot in (1, 3, 0, 2):
        q_gain_part += second_pass(slot)

    dkv_copies = []
    for slot in (2, 1, 3):
        here = slice(slot * rows, (slot + 1) * rows)
        dkv_send[slot] = acc[here, :].astype(jnp.bfloat16)
        one = copy(dkv_send.at[slot], dkv_in.at[slot], along_x(SIDE - slot))
        dkv_copies.append(one)
        one.start()
    k_gain_part = jnp.zeros((1, width), jnp.float32)
    for head in range(heads):
        k_gain_part += jnp.sum(acc[:, cols(head)] * k_unit[:, cols(head)], axis=0, keepdims=True)

    line = lax.broadcasted_iota(jnp.int32, (8, width), 0)
    part = jnp.where(line == 0, q_gain_part, jnp.where(line == 1, k_gain_part, 0.0))

    def restore(grad, unit, inverse, gain):
        scaled = grad * gain
        return inverse * (scaled - unit * jnp.mean(scaled * unit, axis=1, keepdims=True))

    def finish_q():
        for one in dq_copies:
            one.wait_recv()
        for head in range(heads):
            grad = dq_own[:, cols(head)]
            for slot in range(1, SIDE):
                grad += dq_in[slot, :, cols(head)].astype(jnp.float32)
            dq_out[:, cols(head)] = restore(
                grad, q_unit[0, :, cols(head)], q_inverse[:, cols(head)], q_gain_ref[...]
            ).astype(jnp.bfloat16)

    def finish_k():
        for one in dkv_copies:
            one.wait_recv()
        for head in range(heads):
            there = slice(flat + head * width, flat + (head + 1) * width)
            grad = acc[:rows, cols(head)]
            total = acc[:rows, there]
            for slot in range(1, SIDE):
                grad += dkv_in[slot, :, cols(head)].astype(jnp.float32)
                total += dkv_in[slot, :, there].astype(jnp.float32)
            dk_out[:, cols(head)] = restore(
                grad, k_unit[:rows, cols(head)], k_inverse[:, cols(head)], k_gain_ref[...]
            ).astype(jnp.bfloat16)
            dv_out[:, cols(head)] = total.astype(jnp.bfloat16)

    stages = (
        (gain_dp, n_dp, dp, along_dp, None),
        (gain_x, SIDE, x, along_x, finish_q),
        (gain_z, SIDE, z, along_z, finish_k),
        (gain_tp, n_tp, tp, along_tp, None),
    )
    for buffer, size, place, device, between in stages:
        buffer[place] = part
        copies = []
        for step in range(1, size):
            one = copy(buffer.at[place], buffer.at[place], device(step))
            copies.append(one)
            one.start()
        if between is not None:
            between()
        for one in copies:
            one.wait_recv()
        part = buffer[0]
        for index in range(1, size):
            part += buffer[index]
    gain_out[...] = part / length
    for one in started:
        one.wait_send()


def local(q_raw, k_raw, value, d_out, q_gain, k_gain):
    width = q_gain.shape[0]
    rows, flat = q_raw.shape[1:]
    heads = flat // width
    n_ctx, n_tp, n_dp = (lax.axis_size(name) for name in ("ctx", "tp", "dp"))
    keys = SIDE * rows
    low, full = jnp.bfloat16, jnp.float32
    copies = 12 + 12 + 3 + 3 + 2 * (SIDE - 1) + n_dp - 1 + n_tp - 1
    sizes = (n_tp, n_dp, heads, n_ctx * rows)
    block = jax.ShapeDtypeStruct((rows, flat), low)
    vmem = pl.BlockSpec(memory_space=pltpu.VMEM)
    dq, dk, dv, gains = pl.pallas_call(
        functools.partial(kernel, sizes),
        out_shape=(block, block, block, jax.ShapeDtypeStruct((8, width), full)),
        in_specs=[vmem] * 6,
        out_specs=(vmem,) * 4,
        scratch_shapes=[
            pltpu.VMEM((SIDE, rows, flat), low),
            pltpu.VMEM((SIDE, rows, flat), low),
            pltpu.VMEM((SIDE, rows, flat), low),
            pltpu.VMEM((SIDE, rows, flat), low),
            pltpu.VMEM((SIDE, rows, flat), low),
            pltpu.VMEM((SIDE, rows, flat), full),
            pltpu.VMEM((rows, flat), full),
            pltpu.VMEM((keys, flat), low),
            pltpu.VMEM((keys, flat), full),
            pltpu.VMEM((rows, flat), full),
            pltpu.VMEM((heads, width, keys), low),
            pltpu.VMEM((SIDE, heads, keys, rows), full),
            pltpu.VMEM((SIDE, heads, keys, rows), full),
            pltpu.VMEM((SIDE, 8, rows), full),
            pltpu.VMEM((SIDE, SIDE, 8, rows), full),
            pltpu.VMEM((keys, 2 * flat), full),
            pltpu.VMEM((SIDE, rows, 2 * flat), low),
            pltpu.VMEM((SIDE, rows, 2 * flat), low),
            pltpu.VMEM((rows, flat), full),
            pltpu.VMEM((SIDE, rows, flat), low),
            pltpu.VMEM((SIDE, rows, flat), low),
            pltpu.VMEM((n_dp, 8, width), full),
            pltpu.VMEM((SIDE, 8, width), full),
            pltpu.VMEM((SIDE, 8, width), full),
            pltpu.VMEM((n_tp, 8, width), full),
            pltpu.SemaphoreType.DMA((copies,)),
            pltpu.SemaphoreType.DMA((copies,)),
        ],
        compiler_params=pltpu.CompilerParams(collective_id=0, has_side_effects=True),
    )(
        q_raw[0],
        k_raw[0],
        value[0],
        d_out[0],
        q_gain[None],
        k_gain[None],
    )
    return (dq[None], dk[None], dv[None], gains[0], gains[1])


def solution(mesh):
    split = P("dp", "ctx", "tp")
    return jax.shard_map(
        local,
        mesh=mesh,
        in_specs=(split, split, split, split, P(), P()),
        out_specs=(split, split, split, P(), P()),
        check_vma=False,
    )
```

time: 364 us -> 56.4 us (0.15)
  waiting for transfers between devices: 203 us -> 0 us
  blocking collectives: 96.3 us -> 0 us
  Pallas kernels: 0 us -> 50.9 us
  local copies, waits for them, and re-layouts: 26.5 us -> 4.27 us
  between operations: 14 us -> 0.64 us
  other arithmetic: 10.5 us -> 0 us
  matrix products: 9.47 us -> 0 us
    all_gather x2 -> x0, waiting for transfers between devices: 120 us -> none  [the longest x1 60.4 us: local(): lax.all_gather(own_value, 'ctx', axis=0, tiled=True)]
    psum x1 -> x0, blocking collectives: 96.3 us -> none  [local(): lax.psum((q_gain_part, k_gain_part), ('ctx', 'tp', 'dp'))]
    reduce_scatter x1 -> x0, waiting for transfers between devices: 82.7 us -> none  [local(): lax.psum_scatter(lax.map(one_block, jnp.arange(lax.axis_size('ctx') * row...]
    pallas_call x0 -> x1, Pallas kernels: none -> 50.9 us  [local(): pl.pallas_call(functools.partial(kernel, sizes), out_shape=(block, block,...]
    dynamic_slice x16 -> x0, local copies, waits for them, and re-layouts: 14.3 us -> none  [the longest x12 12 us: key_slice(): lax.dynamic_slice_in_dim(all_values, begin, size, 0)]
    dot_general x28 -> x0, matrix products: 9.47 us -> none  [the longest x8 2.32 us: block_weights(): jnp.einsum('qhd,khd->hqk', query_normed, key_normed, preferred_element_ty...]
    convert_element_type x4 -> x0, local copies, waits for them, and re-layouts: 6.73 us -> none  [the longest x1 4.14 us: local(): summed = lax.psum_scatter(lax.map(one_block, jnp.arange(lax.axis_size('ct...]
  transfers between devices with their start and end apart: 3 -> 0, of which waited for: 3 -> 0; matrix products, arithmetic and copies ran while one was open for 4% -> 0% of each run, Pallas kernels for 0% -> 0%
where the time goes in v1:
time: 56.4 us; the launch traced here: 55.8 us
  Pallas kernels  50.9 us (90%)
  local copies, waits for them, and re-layouts  4.27 us (8%)
  between operations  0.64 us (1%)
    pallas_call x1, Pallas kernels, local(): pl.pallas_call(functools.partial(kernel, sizes), out_shape=(block, block,...  50.9 us
    unnamed x7, local copies, waits for them, and re-layouts  3 us
    squeeze x1, local copies, waits for them, and re-layouts, local(): return (dq[None], dk[None], dv[None], gains[0], gains[1])  1.27 us

profile of v1, /device:TPU:1, one launch (start us, length us, event | category | flops | bytes accessed | tf_op | source)
XLA Modules:
  0.0 55.8 jit_solution(9420462767098267917)
XLA Ops:
  0.6 50.9 %shard_map.101 = (bf16[128,256]{1,0:T(8,128)(2,1)}, bf16[128,256]{1,0:T(8,128)(2,1)}, bf16[128,256]{1,0:T(8,128)(2,1)}, f32[8,128]{1,0:T(8,128)}) custom-call(bf16[128,256]{1,0:T(8,128)(2,1)} %bitcast.16, bf16[128,256]{1,0:T(8,128)(2,1)} %bitcast.17, bf16[128,256]{1,0:T(8,128)(2,1)} %bitcast.18, bf16[128,256]{1,0:T(8,128)(2,1)} %bitcast.19, ...), custom_call_target="tpu_custom_call" | custom-call | tf_op jit(solution)/shard_map/pallas_call | solution.py:338
  51.5 1.3 %slice_bitcast_fusion = (f32[128]{0:T(128)}, f32[128]{0:T(128)}) fusion(f32[8,128]{1,0:T(8,128)} %get-tuple-element.12), kind=kLoop, calls=%fused_computation | loop fusion | bytes 2048 | tf_op jit(solution)/shard_map/squeeze | solution.py:381
  52.8 0.0 copy-start.1
  52.8 1.5 %copy.14 = bf16[1,128,256]{2,1,0:T(8,128)(2,1)} copy(bf16[1,128,256]{2,1,0:T(8,128)(2,1)} %bitcast.15) | data formatting | bytes 131072
  54.3 0.0 copy-done.1
  54.3 0.0 copy-start
  54.3 0.6 %copy.15 = bf16[1,128,256]{2,1,0:T(8,128)(2,1)} copy(bf16[1,128,256]{2,1,0:T(8,128)(2,1)S(1)} %bitcast.14) | data formatting | bytes 131072
  55.0 0.2 copy-done
  55.2 0.6 %copy.16 = bf16[1,128,256]{2,1,0:T(8,128)(2,1)} copy(bf16[1,128,256]{2,1,0:T(8,128)(2,1)S(1)} %bitcast.13) | data formatting | bytes 131072
Async XLA Ops:
  52.8 1.5 %copy-start.1 = (bf16[128,256]{1,0:T(8,128)(2,1)S(1)}, bf16[128,256]{1,0:T(8,128)(2,1)}, u32[]{:S(2)}) copy-start(bf16[128,256]{1,0:T(8,128)(2,1)} %get-tuple-element.10) | copy-start | bytes 196612
  54.3 0.9 %copy-start = (bf16[128,256]{1,0:T(8,128)(2,1)S(1)}, bf16[128,256]{1,0:T(8,128)(2,1)}, u32[]{:S(2)}) copy-start(bf16[128,256]{1,0:T(8,128)(2,1)} %get-tuple-element.11) | copy-start | bytes 196612

commit v2 on v1

v2 whole, which is shorter than its diff:
```python
import functools

import jax
import jax.numpy as jnp
from jax import lax
from jax.experimental import pallas as pl
from jax.experimental.pallas import tpu as pltpu
from jax.sharding import PartitionSpec as P

EPSILON = 1e-06
SIDE = 4
MESH = pl.DeviceIdType.MESH


def kernel(
    sizes,
    q_hbm,
    k_hbm,
    v_hbm,
    o_hbm,
    q_gain_hbm,
    k_gain_hbm,
    dq_out,
    dk_out,
    dv_out,
    gain_out,
    q_gain_ref,
    k_gain_ref,
    q_raw,
    k_raw,
    v_all,
    o_all,
    q_normed,
    q_unit,
    q_inverse,
    k_normed,
    k_unit,
    k_inverse,
    k_turned,
    expo,
    dprob,
    stat_own,
    stat_in,
    dk_acc,
    dv_acc,
    dk_send,
    dv_send,
    dk_in,
    dv_in,
    dk_far,
    dv_far,
    dq_full,
    dq_send,
    dq_in,
    dq_far,
    gain_tp,
    gain_z,
    gain_x,
    load_sem,
    send_sem,
    recv_sem,
):
    n_tp, n_dp, heads, length = sizes
    rows = q_hbm.shape[0]
    width = q_gain_hbm.shape[1]
    keys = SIDE * rows
    scale = width ** (-0.5)
    ctx = lax.axis_index("ctx")
    tp = lax.axis_index("tp")
    dp = lax.axis_index("dp")
    x = lax.rem(ctx, SIDE)
    z = ctx // SIDE

    def along_x(step):
        return {"ctx": z * SIDE + lax.rem(x + step, SIDE), "tp": tp, "dp": dp}

    def along_z(step):
        return {"ctx": lax.rem(z + step, SIDE) * SIDE + x, "tp": tp, "dp": dp}

    def along_z_dp(step):
        place = lax.rem(z + step // n_dp, SIDE) * SIDE + x
        return {"ctx": place, "tp": tp, "dp": lax.rem(dp + step % n_dp, n_dp)}

    def along_tp(step):
        return {"ctx": ctx, "tp": lax.rem(tp + step, n_tp), "dp": dp}

    barrier = pltpu.get_barrier_semaphore()
    partners = (
        [along_z_dp(step) for step in range(1, SIDE * n_dp)]
        + [along_tp(step) for step in range(1, n_tp)]
        + [along_x(step) for step in range(1, SIDE)]
    )
    for partner in partners:
        pl.semaphore_signal(barrier, inc=1, device_id=partner, device_id_type=MESH)

    loads = [
        pltpu.make_async_copy(src, dst, load_sem.at[index])
        for index, (src, dst) in enumerate(
            (
                (q_gain_hbm, q_gain_ref),
                (k_gain_hbm, k_gain_ref),
                (k_hbm, k_raw.at[0]),
                (q_hbm, q_raw.at[0]),
                (v_hbm, v_all.at[0]),
                (o_hbm, o_all.at[0]),
            )
        )
    ]
    for one in loads:
        one.start()

    count = [0]
    started = []

    def copy(src, dst, device):
        index = count[0]
        count[0] += 1
        one = pltpu.make_async_remote_copy(
            src_ref=src,
            dst_ref=dst,
            send_sem=send_sem.at[index],
            recv_sem=recv_sem.at[index],
            device_id=device,
            device_id_type=MESH,
        )
        started.append(one)
        return one

    def cols(head):
        return slice(head * width, (head + 1) * width)

    pl.semaphore_wait(barrier, len(partners))

    q_up = copy(q_hbm, q_raw.at[1], along_z(1))
    q_down = copy(q_hbm, q_raw.at[3], along_z(3))
    o_up = copy(o_hbm, o_all.at[1], along_z(1))
    o_down = copy(o_hbm, o_all.at[3], along_z(3))
    k_up = copy(k_hbm, k_raw.at[1], along_x(1))
    k_down = copy(k_hbm, k_raw.at[3], along_x(3))
    v_up = copy(v_hbm, v_all.at[1], along_x(1))
    v_down = copy(v_hbm, v_all.at[3], along_x(3))
    for one in (q_up, o_down, k_up, v_down, o_up, q_down, v_up, k_down):
        one.start()
    q_far = copy(q_raw.at[1], q_raw.at[2], along_z(1))
    o_far = copy(o_all.at[3], o_all.at[2], along_z(3))
    k_far = copy(k_raw.at[1], k_raw.at[2], along_x(1))
    v_far = copy(v_all.at[3], v_all.at[2], along_x(3))

    dk_acc[...] = jnp.zeros_like(dk_acc)
    dv_acc[...] = jnp.zeros_like(dv_acc)
    stat_own[...] = jnp.zeros_like(stat_own)
    for one in loads:
        one.wait()

    def norm_q(slot):
        for head in range(heads):
            values = q_raw[slot, :, cols(head)].astype(jnp.float32)
            inverse = lax.rsqrt(jnp.mean(values * values, axis=1, keepdims=True) + EPSILON)
            unit = values * inverse
            q_unit[slot, :, cols(head)] = unit
            q_normed[slot, :, cols(head)] = (unit * q_gain_ref[...]).astype(jnp.bfloat16)
            if slot == 0:
                q_inverse[:, cols(head)] = jnp.broadcast_to(inverse, (rows, width))

    def norm_k(slot):
        here = slice(slot * rows, (slot + 1) * rows)
        for head in range(heads):
            values = k_raw[slot, :, cols(head)].astype(jnp.float32)
            inverse = lax.rsqrt(jnp.mean(values * values, axis=1, keepdims=True) + EPSILON)
            unit = values * inverse
            normed = (unit * k_gain_ref[...]).astype(jnp.bfloat16)
            k_unit[here, cols(head)] = unit
            k_normed[here, cols(head)] = normed
            k_turned[head, :, here] = normed.T
            if slot == 0:
                k_inverse[:, cols(head)] = jnp.broadcast_to(inverse, (rows, width))

    norm_q(0)
    norm_k(0)

    k_up.wait_recv()
    k_far.start()
    v_down.wait_recv()
    v_far.start()
    norm_k(1)
    k_down.wait_recv()
    norm_k(3)
    v_up.wait_recv()
    q_up.wait_recv()
    q_far.start()
    o_down.wait_recv()
    o_far.start()
    k_far.wait_recv()
    norm_k(2)
    v_far.wait_recv()

    def contract_last(left, right):
        return lax.dot_general(
            left, right, (((1,), (1,)), ((), ())), preferred_element_type=jnp.float32
        )

    stat_copies = {}

    def first_pass(slot):
        for head in range(heads):
            scores = (
                contract_last(k_normed[:, cols(head)], q_normed[slot, :, cols(head)]) * scale
            )
            top = jnp.max(scores, axis=0, keepdims=True)
            weights = jnp.exp(scores - top)
            slopes = contract_last(
                v_all[:, :, cols(head)].reshape(keys, width), o_all[slot, :, cols(head)]
            )
            expo[slot, head] = weights
            dprob[slot, head] = slopes
            stat_own[slot, 3 * head : 3 * head + 1] = top
            stat_own[slot, 3 * head + 1 : 3 * head + 2] = jnp.sum(weights, axis=0, keepdims=True)
            stat_own[slot, 3 * head + 2 : 3 * head + 3] = jnp.sum(
                weights * slopes, axis=0, keepdims=True
            )
        for step in (2, 1, 3):
            there = (slot + step) % SIDE
            one = copy(stat_own.at[slot], stat_in.at[there, step], along_z(step))
            stat_copies[there, step] = one
            one.start()

    first_pass(0)
    o_up.wait_recv()
    norm_q(1)
    first_pass(1)
    q_down.wait_recv()
    norm_q(3)
    first_pass(3)
    q_far.wait_recv()
    norm_q(2)
    o_far.wait_recv()
    first_pass(2)

    def second_pass(slot):
        for step in range(1, SIDE):
            stat_copies[slot, step].wait_recv()
        part = jnp.zeros((1, width), jnp.float32)
        for head in range(heads):
            tops = [stat_own[slot, 3 * head : 3 * head + 1]]
            totals = [stat_own[slot, 3 * head + 1 : 3 * head + 2]]
            weighted = [stat_own[slot, 3 * head + 2 : 3 * head + 3]]
            for step in range(1, SIDE):
                tops.append(stat_in[slot, step, 3 * head : 3 * head + 1])
                totals.append(stat_in[slot, step, 3 * head + 1 : 3 * head + 2])
                weighted.append(stat_in[slot, step, 3 * head + 2 : 3 * head + 3])
            top = functools.reduce(jnp.maximum, tops)
            factors = [jnp.exp(one - top) for one in tops]
            total = sum(one * factor for one, factor in zip(totals, factors))
            delta = sum(one * factor for one, factor in zip(weighted, factors)) / total
            prob = expo[slot, head] * (factors[0] / total)
            dscore = (prob * (dprob[slot, head] - delta) * scale).astype(jnp.bfloat16)
            prob_low = prob.astype(jnp.bfloat16)
            dq = jnp.dot(k_turned[head], dscore, preferred_element_type=jnp.float32).T
            part += jnp.sum(dq * q_unit[slot, :, cols(head)], axis=0, keepdims=True)
            dq_full[slot, head] = dq
            dk_acc[:, cols(head)] += jnp.dot(
                dscore, q_normed[slot, :, cols(head)], preferred_element_type=jnp.float32
            )
            dv_acc[:, cols(head)] += jnp.dot(
                prob_low, o_all[slot, :, cols(head)], preferred_element_type=jnp.float32
            )
        return part

    def via(head):
        return 1 if head % 2 == 0 else 3

    def start(src, dst, device):
        one = copy(src, dst, device)
        one.start()
        return one

    dq_far_copies, dq_copies = [], []
    q_gain_part = second_pass(2)
    for head in range(heads):
        dq_send[2, head] = dq_full[2, head].astype(jnp.bfloat16)
        device = along_z(SIDE - via(head))
        dq_far_copies.append(start(dq_send.at[2, head], dq_far.at[head], device))
    for slot in (1, 3):
        q_gain_part += second_pass(slot)
        for head in range(heads):
            if via(head) != slot:
                dq_send[slot, head] = dq_full[slot, head].astype(jnp.bfloat16)
                device = along_z(SIDE - slot)
                dq_copies.append(start(dq_send.at[slot, head], dq_in.at[slot, head], device))
    q_gain_part += second_pass(0)

    def block(slot):
        return slice(slot * rows, (slot + 1) * rows)

    dk_send[2] = dk_acc[block(2), :].astype(jnp.bfloat16)
    dk_far_copy = start(dk_send.at[2], dk_far, along_x(3))
    dv_send[2] = dv_acc[block(2), :].astype(jnp.bfloat16)
    dv_far_copy = start(dv_send.at[2], dv_far, along_x(1))
    dk_send[3] = dk_acc[block(3), :].astype(jnp.bfloat16)
    dk_near = start(dk_send.at[3], dk_in.at[3], along_x(1))
    dv_send[1] = dv_acc[block(1), :].astype(jnp.bfloat16)
    dv_near = start(dv_send.at[1], dv_in.at[1], along_x(3))

    k_gain_part = jnp.zeros((1, width), jnp.float32)
    for head in range(heads):
        k_gain_part += jnp.sum(
            dk_acc[:, cols(head)] * k_unit[:, cols(head)], axis=0, keepdims=True
        )
    line = lax.broadcasted_iota(jnp.int32, (8, width), 0)
    part = jnp.where(line == 0, q_gain_part, jnp.where(line == 1, k_gain_part, 0.0))

    def spread(buffer, size, place, device, part):
        buffer[place] = part
        return [
            start(buffer.at[place], buffer.at[place], device(step)) for step in range(1, size)
        ]

    def gathered(buffer, size, copies):
        for one in copies:
            one.wait_recv()
        part = buffer[0]
        for index in range(1, size):
            part += buffer[index]
        return part

    gain_copies = spread(gain_tp, n_tp, tp, along_tp, part)

    for head in range(heads):
        slot = via(head)
        dq_far_copies[head].wait_recv()
        total = dq_full[slot, head] + dq_far[head].astype(jnp.float32)
        dq_send[slot, head] = total.astype(jnp.bfloat16)
        device = along_z(SIDE - slot)
        dq_copies.append(start(dq_send.at[slot, head], dq_in.at[slot, head], device))

    dk_far_copy.wait_recv()
    total = dk_acc[block(1), :] + dk_far[...].astype(jnp.float32)
    dk_send[1] = total.astype(jnp.bfloat16)
    dk_last = start(dk_send.at[1], dk_in.at[1], along_x(3))
    dv_far_copy.wait_recv()
    total = dv_acc[block(3), :] + dv_far[...].astype(jnp.float32)
    dv_send[3] = total.astype(jnp.bfloat16)
    dv_last = start(dv_send.at[3], dv_in.at[3], along_x(1))

    part = gathered(gain_tp, n_tp, gain_copies)
    gain_copies = spread(gain_z, SIDE * n_dp, z * n_dp + dp, along_z_dp, part)

    def restore(grad, unit, inverse, gain):
        scaled = grad * gain
        return inverse * (scaled - unit * jnp.mean(scaled * unit, axis=1, keepdims=True))

    for one in dq_copies:
        one.wait_recv()
    for head in range(heads):
        grad = dq_full[0, head]
        for slot in (1, 3):
            grad += dq_in[slot, head].astype(jnp.float32)
        dq_out[:, cols(head)] = restore(
            grad, q_unit[0, :, cols(head)], q_inverse[:, cols(head)], q_gain_ref[...]
        ).astype(jnp.bfloat16)

    part = gathered(gain_z, SIDE * n_dp, gain_copies)
    gain_copies = spread(gain_x, SIDE, x, along_x, part)

    for one in (dk_near, dv_near, dk_last, dv_last):
        one.wait_recv()
    for head in range(heads):
        grad = dk_acc[block(0), cols(head)]
        total = dv_acc[block(0), cols(head)]
        for slot in (1, 3):
            grad += dk_in[slot, :, cols(head)].astype(jnp.float32)
            total += dv_in[slot, :, cols(head)].astype(jnp.float32)
        dk_out[:, cols(head)] = restore(
            grad, k_unit[block(0), cols(head)], k_inverse[:, cols(head)], k_gain_ref[...]
        ).astype(jnp.bfloat16)
        dv_out[:, cols(head)] = total.astype(jnp.bfloat16)

    gain_out[...] = gathered(gain_x, SIDE, gain_copies) / length
    for one in started:
        one.wait_send()


def local(q_raw, k_raw, value, d_out, q_gain, k_gain):
    width = q_gain.shape[0]
    rows, flat = q_raw.shape[1:]
    heads = flat // width
    n_ctx, n_tp, n_dp = (lax.axis_size(name) for name in ("ctx", "tp", "dp"))
    keys = SIDE * rows
    low, full = jnp.bfloat16, jnp.float32
    copies = 12 + 12 + 3 * heads + 6 + SIDE * n_dp - 1 + n_tp - 1 + SIDE - 1
    sizes = (n_tp, n_dp, heads, n_ctx * rows)
    block = jax.ShapeDtypeStruct((rows, flat), low)
    vmem = pl.BlockSpec(memory_space=pltpu.VMEM)
    dq, dk, dv, gains = pl.pallas_call(
        functools.partial(kernel, sizes),
        out_shape=(block, block, block, jax.ShapeDtypeStruct((8, width), full)),
        in_specs=[pl.BlockSpec(memory_space=pl.ANY)] * 6,
        out_specs=(vmem,) * 4,
        scratch_shapes=[
            pltpu.VMEM((1, width), full),
            pltpu.VMEM((1, width), full),
            pltpu.VMEM((SIDE, rows, flat), low),
            pltpu.VMEM((SIDE, rows, flat), low),
            pltpu.VMEM((SIDE, rows, flat), low),
            pltpu.VMEM((SIDE, rows, flat), low),
            pltpu.VMEM((SIDE, rows, flat), low),
            pltpu.VMEM((SIDE, rows, flat), full),
            pltpu.VMEM((rows, flat), full),
            pltpu.VMEM((keys, flat), low),
            pltpu.VMEM((keys, flat), full),
            pltpu.VMEM((rows, flat), full),
            pltpu.VMEM((heads, width, keys), low),
            pltpu.VMEM((SIDE, heads, keys, rows), full),
            pltpu.VMEM((SIDE, heads, keys, rows), full),
            pltpu.VMEM((SIDE, 8, rows), full),
            pltpu.VMEM((SIDE, SIDE, 8, rows), full),
            pltpu.VMEM((keys, flat), full),
            pltpu.VMEM((keys, flat), full),
            pltpu.VMEM((SIDE, rows, flat), low),
            pltpu.VMEM((SIDE, rows, flat), low),
            pltpu.VMEM((SIDE, rows, flat), low),
            pltpu.VMEM((SIDE, rows, flat), low),
            pltpu.VMEM((rows, flat), low),
            pltpu.VMEM((rows, flat), low),
            pltpu.VMEM((SIDE, heads, rows, width), full),
            pltpu.VMEM((SIDE, heads, rows, width), low),
            pltpu.VMEM((SIDE, heads, rows, width), low),
            pltpu.VMEM((heads, rows, width), low),
            pltpu.VMEM((n_tp, 8, width), full),
            pltpu.VMEM((SIDE * n_dp, 8, width), full),
            pltpu.VMEM((SIDE, 8, width), full),
            pltpu.SemaphoreType.DMA((6,)),
            pltpu.SemaphoreType.DMA((copies,)),
            pltpu.SemaphoreType.DMA((copies,)),
        ],
        compiler_params=pltpu.CompilerParams(collective_id=0, has_side_effects=True),
    )(
        q_raw[0],
        k_raw[0],
        value[0],
        d_out[0],
        q_gain[None],
        k_gain[None],
    )
    return (dq[None], dk[None], dv[None], gains[0], gains[1])


def solution(mesh):
    split = P("dp", "ctx", "tp")
    return jax.shard_map(
        local,
        mesh=mesh,
        in_specs=(split, split, split, split, P(), P()),
        out_specs=(split, split, split, P(), P()),
        check_vma=False,
    )
```

time: 56.4 us -> 53.3 us (0.945)
  Pallas kernels: 50.9 us -> 48.2 us
    pallas_call x1, Pallas kernels: 50.9 us -> 48.2 us  [local(): pl.pallas_call(functools.partial(kernel, sizes), out_shape=(block, block,...]
where the time goes in v2:
time: 53.3 us; the launch traced here: 53.1 us
  Pallas kernels  48.2 us (90%)
  local copies, waits for them, and re-layouts  4.27 us (8%)
  between operations  0.64 us (1%)
    pallas_call x1, Pallas kernels, local(): pl.pallas_call(functools.partial(kernel, sizes), out_shape=(block, block,...  48.2 us
    unnamed x7, local copies, waits for them, and re-layouts  3 us
    squeeze x1, local copies, waits for them, and re-layouts, local(): return (dq[None], dk[None], dv[None], gains[0], gains[1])  1.27 us

profile of v2, /device:TPU:1, one launch (start us, length us, event | category | flops | bytes accessed | tf_op | source)
XLA Modules:
  0.0 53.1 jit_solution(10624007743536600838)
XLA Ops:
  0.6 48.2 %shard_map.101 = (bf16[128,256]{1,0:T(8,128)(2,1)}, bf16[128,256]{1,0:T(8,128)(2,1)}, bf16[128,256]{1,0:T(8,128)(2,1)}, f32[8,128]{1,0:T(8,128)}) custom-call(bf16[128,256]{1,0:T(8,128)(2,1)} %bitcast.16, bf16[128,256]{1,0:T(8,128)(2,1)} %bitcast.17, bf16[128,256]{1,0:T(8,128)(2,1)} %bitcast.18, bf16[128,256]{1,0:T(8,128)(2,1)} %bitcast.19, ...), custom_call_target="tpu_custom_call" | custom-call | tf_op jit(solution)/shard_map/pallas_call | solution.py:394
  48.8 1.3 %slice_bitcast_fusion = (f32[128]{0:T(128)}, f32[128]{0:T(128)}) fusion(f32[8,128]{1,0:T(8,128)} %get-tuple-element.12), kind=kLoop, calls=%fused_computation | loop fusion | bytes 2048 | tf_op jit(solution)/shard_map/squeeze | solution.py:445
  50.1 0.0 copy-start.1
  50.1 1.5 %copy.14 = bf16[1,128,256]{2,1,0:T(8,128)(2,1)} copy(bf16[1,128,256]{2,1,0:T(8,128)(2,1)} %bitcast.15) | data formatting | bytes 131072
  51.6 0.0 copy-done.1
  51.6 0.0 copy-start
  51.6 0.6 %copy.15 = bf16[1,128,256]{2,1,0:T(8,128)(2,1)} copy(bf16[1,128,256]{2,1,0:T(8,128)(2,1)S(1)} %bitcast.14) | data formatting | bytes 131072
  52.2 0.2 copy-done
  52.4 0.6 %copy.16 = bf16[1,128,256]{2,1,0:T(8,128)(2,1)} copy(bf16[1,128,256]{2,1,0:T(8,128)(2,1)S(1)} %bitcast.13) | data formatting | bytes 131072
Async XLA Ops:
  50.1 1.5 %copy-start.1 = (bf16[128,256]{1,0:T(8,128)(2,1)S(1)}, bf16[128,256]{1,0:T(8,128)(2,1)}, u32[]{:S(2)}) copy-start(bf16[128,256]{1,0:T(8,128)(2,1)} %get-tuple-element.10) | copy-start | bytes 196612
  51.6 0.9 %copy-start = (bf16[128,256]{1,0:T(8,128)(2,1)S(1)}, bf16[128,256]{1,0:T(8,128)(2,1)}, u32[]{:S(2)}) copy-start(bf16[128,256]{1,0:T(8,128)(2,1)} %get-tuple-element.11) | copy-start | bytes 196612

commit v3 on v2

--- a/solution.py
+++ b/solution.py
@@ -20,9 +20,7 @@
     o_hbm,
     q_gain_hbm,
     k_gain_hbm,
-    dq_out,
-    dk_out,
-    dv_out,
+    grad_out,
     gain_out,
     q_gain_ref,
     k_gain_ref,
@@ -306,8 +304,7 @@
         k_gain_part += jnp.sum(
             dk_acc[:, cols(head)] * k_unit[:, cols(head)], axis=0, keepdims=True
         )
-    line = lax.broadcasted_iota(jnp.int32, (8, width), 0)
-    part = jnp.where(line == 0, q_gain_part, jnp.where(line == 1, k_gain_part, 0.0))
+    part = jnp.concatenate([q_gain_part, k_gain_part], axis=0)
 
     def spread(buffer, size, place, device, part):
         buffer[place] = part
@@ -332,6 +329,9 @@
         dq_send[slot, head] = total.astype(jnp.bfloat16)
         device = along_z(SIDE - slot)
         dq_copies.append(start(dq_send.at[slot, head], dq_in.at[slot, head], device))
+
+    part = gathered(gain_tp, n_tp, gain_copies)
+    gain_copies = spread(gain_z, SIDE * n_dp, z * n_dp + dp, along_z_dp, part)
 
     dk_far_copy.wait_recv()
     total = dk_acc[block(1), :] + dk_far[...].astype(jnp.float32)
@@ -342,9 +342,6 @@
     dv_send[3] = total.astype(jnp.bfloat16)
     dv_last = start(dv_send.at[3], dv_in.at[3], along_x(1))
 
-    part = gathered(gain_tp, n_tp, gain_copies)
-    gain_copies = spread(gain_z, SIDE * n_dp, z * n_dp + dp, along_z_dp, part)
-
     def restore(grad, unit, inverse, gain):
         scaled = grad * gain
         return inverse * (scaled - unit * jnp.mean(scaled * unit, axis=1, keepdims=True))
@@ -355,7 +352,7 @@
         grad = dq_full[0, head]
         for slot in (1, 3):
             grad += dq_in[slot, head].astype(jnp.float32)
-        dq_out[:, cols(head)] = restore(
+        grad_out[0, :, cols(head)] = restore(
             grad, q_unit[0, :, cols(head)], q_inverse[:, cols(head)], q_gain_ref[...]
         ).astype(jnp.bfloat16)
 
@@ -370,10 +367,10 @@
         for slot in (1, 3):
             grad += dk_in[slot, :, cols(head)].astype(jnp.float32)
             total += dv_in[slot, :, cols(head)].astype(jnp.float32)
-        dk_out[:, cols(head)] = restore(
+        grad_out[1, :, cols(head)] = restore(
             grad, k_unit[block(0), cols(head)], k_inverse[:, cols(head)], k_gain_ref[...]
         ).astype(jnp.bfloat16)
-        dv_out[:, cols(head)] = total.astype(jnp.bfloat16)
+        grad_out[2, :, cols(head)] = total.astype(jnp.bfloat16)
 
     gain_out[...] = gathered(gain_x, SIDE, gain_copies) / length
     for one in started:
@@ -389,13 +386,13 @@
     low, full = jnp.bfloat16, jnp.float32
     copies = 12 + 12 + 3 * heads + 6 + SIDE * n_dp - 1 + n_tp - 1 + SIDE - 1
     sizes = (n_tp, n_dp, heads, n_ctx * rows)
-    block = jax.ShapeDtypeStruct((rows, flat), low)
+    block = jax.ShapeDtypeStruct((3, rows, flat), low)
     vmem = pl.BlockSpec(memory_space=pltpu.VMEM)
-    dq, dk, dv, gains = pl.pallas_call(
+    grads, gains = pl.pallas_call(
         functools.partial(kernel, sizes),
-        out_shape=(block, block, block, jax.ShapeDtypeStruct((8, width), full)),
+        out_shape=(block, jax.ShapeDtypeStruct((2, width), full)),
         in_specs=[pl.BlockSpec(memory_space=pl.ANY)] * 6,
-        out_specs=(vmem,) * 4,
+        out_specs=(vmem,) * 2,
         scratch_shapes=[
             pltpu.VMEM((1, width), full),
             pltpu.VMEM((1, width), full),
@@ -426,9 +423,9 @@
             pltpu.VMEM((SIDE, heads, rows, width), low),
             pltpu.VMEM((SIDE, heads, rows, width), low),
             pltpu.VMEM((heads, rows, width), low),
-            pltpu.VMEM((n_tp, 8, width), full),
-            pltpu.VMEM((SIDE * n_dp, 8, width), full),
-            pltpu.VMEM((SIDE, 8, width), full),
+            pltpu.VMEM((n_tp, 2, width), full),
+            pltpu.VMEM((SIDE * n_dp, 2, width), full),
+            pltpu.VMEM((SIDE, 2, width), full),
             pltpu.SemaphoreType.DMA((6,)),
             pltpu.SemaphoreType.DMA((copies,)),
             pltpu.SemaphoreType.DMA((copies,)),
@@ -442,7 +439,7 @@
         q_gain[None],
         k_gain[None],
     )
-    return (dq[None], dk[None], dv[None], gains[0], gains[1])
+    return (grads[0:1], grads[1:2], grads[2:3], gains[0], gains[1])
 
 
 def solution(mesh):

time: 53.3 us -> 51.2 us (0.961)
  local copies, waits for them, and re-layouts: 4.27 us -> 2.76 us
  Pallas kernels: 48.2 us -> 47.6 us
    unnamed x7 -> x2, local copies, waits for them, and re-layouts: 3 us -> 0.66 us
    slice x0 -> x1, local copies, waits for them, and re-layouts: none -> 1.58 us  [local(): return (grads[0:1], grads[1:2], grads[2:3], gains[0], gains[1])]
    squeeze x1, local copies, waits for them, and re-layouts: 1.27 us -> 0.52 us  [local(): return (grads[0:1], grads[1:2], grads[2:3], gains[0], gains[1])]
    pallas_call x1, Pallas kernels: 48.2 us -> 47.6 us  [local(): pl.pallas_call(functools.partial(kernel, sizes), out_shape=(block, jax.Sh...]
where the time goes in v3:
time: 51.2 us; the launch traced here: 51 us
  Pallas kernels  47.6 us (93%)
  local copies, waits for them, and re-layouts  2.76 us (5%)
  between operations  0.64 us (1%)
    pallas_call x1, Pallas kernels, local(): pl.pallas_call(functools.partial(kernel, sizes), out_shape=(block, jax.Sh...  47.6 us
    slice x1, local copies, waits for them, and re-layouts, local(): return (grads[0:1], grads[1:2], grads[2:3], gains[0], gains[1])  1.58 us

profile of v3, /device:TPU:1, one launch (start us, length us, event | category | flops | bytes accessed | tf_op | source)
XLA Modules:
  0.0 51.0 jit_solution(15400969170618424904)
XLA Ops:
  0.6 47.6 %shard_map.101 = (bf16[3,128,256]{2,1,0:T(8,128)(2,1)}, f32[2,128]{1,0:T(2,128)}) custom-call(bf16[128,256]{1,0:T(8,128)(2,1)} %bitcast.10, bf16[128,256]{1,0:T(8,128)(2,1)} %bitcast.11, bf16[128,256]{1,0:T(8,128)(2,1)} %bitcast.12, bf16[128,256]{1,0:T(8,128)(2,1)} %bitcast.13, f32[1,128]{1,0:T(1,128)} %bitcast.14, f32[1,128]{1,0:T(1,128)} %bitcast.15), custom_call_target="tpu_custom_call" | custom-call | tf_op jit(solution)/shard_map/pallas_call | solution.py:391
  48.2 1.6 %fusion = (bf16[1,128,256]{2,1,0:T(8,128)(2,1)}, bf16[1,128,256]{2,1,0:T(8,128)(2,1)}, bf16[1,128,256]{2,1,0:T(8,128)(2,1)}) fusion(bf16[3,128,256]{2,1,0:T(8,128)(2,1)} %get-tuple-element.7), kind=kLoop, calls=%fused_computation.2 | loop fusion | bytes 393216 | tf_op jit(solution)/shard_map/slice | solution.py:442
  49.8 0.0 copy-start
  49.8 0.7 %copy-done = f32[2,128]{1,0:T(2,128)S(1)} copy-done((f32[2,128]{1,0:T(2,128)S(1)}, f32[2,128]{1,0:T(2,128)}, u32[]{:S(2)}) %copy-start) | copy-done | bytes 1048
  50.5 0.5 %slice_bitcast_fusion = (f32[128]{0:T(128)}, f32[128]{0:T(128)}) fusion(f32[2,128]{1,0:T(2,128)S(1)} %copy-done), kind=kLoop, calls=%fused_computation | loop fusion | bytes 2048 | tf_op jit(solution)/shard_map/squeeze | solution.py:442
Async XLA Ops:
  49.8 0.7 %copy-start = (f32[2,128]{1,0:T(2,128)S(1)}, f32[2,128]{1,0:T(2,128)}, u32[]{:S(2)}) copy-start(f32[2,128]{1,0:T(2,128)} %get-tuple-element.8) | copy-start | bytes 3076

commit v4 on v3

--- a/solution.py
+++ b/solution.py
@@ -9,6 +9,7 @@
 
 EPSILON = 1e-06
 SIDE = 4
+CORES = 2
 MESH = pl.DeviceIdType.MESH
 
 
@@ -75,18 +76,38 @@
     def along_z(step):
         return {"ctx": lax.rem(z + step, SIDE) * SIDE + x, "tp": tp, "dp": dp}
 
-    def along_z_dp(step):
-        place = lax.rem(z + step // n_dp, SIDE) * SIDE + x
-        return {"ctx": place, "tp": tp, "dp": lax.rem(dp + step % n_dp, n_dp)}
+    chips = n_dp // CORES
+    ring = SIDE * chips
+    core = lax.rem(dp, CORES)
+    z_place = z * chips + dp // CORES
+
+    def along_ring(step):
+        place = lax.rem(z_place + step, ring)
+        return {
+            "ctx": place // chips * SIDE + x,
+            "tp": tp,
+            "dp": lax.rem(place, chips) * CORES + core,
+        }
+
+    def along_x_core(step):
+        return {
+            "ctx": z * SIDE + lax.rem(x + step // CORES, SIDE),
+            "tp": tp,
+            "dp": dp - core + lax.rem(core + step % CORES, CORES),
+        }
 
     def along_tp(step):
         return {"ctx": ctx, "tp": lax.rem(tp + step, n_tp), "dp": dp}
 
     barrier = pltpu.get_barrier_semaphore()
+
+    def farthest_first(size):
+        return sorted(range(1, size), key=lambda step: -min(step, size - step))
+
     partners = (
-        [along_z_dp(step) for step in range(1, SIDE * n_dp)]
-        + [along_tp(step) for step in range(1, n_tp)]
-        + [along_x(step) for step in range(1, SIDE)]
+        [along_ring(step) for step in farthest_first(ring)]
+        + [along_tp(step) for step in farthest_first(n_tp)]
+        + [along_x_core(step) for step in farthest_first(SIDE * CORES)]
     )
     for partner in partners:
         pl.semaphore_signal(barrier, inc=1, device_id=partner, device_id_type=MESH)
@@ -290,6 +311,30 @@
     def block(slot):
         return slice(slot * rows, (slot + 1) * rows)
 
+    k_gain_part = jnp.zeros((1, width), jnp.float32)
+    for head in range(heads):
+        k_gain_part += jnp.sum(
+            dk_acc[:, cols(head)] * k_unit[:, cols(head)], axis=0, keepdims=True
+        )
+    part = jnp.concatenate([q_gain_part, k_gain_part], axis=0)
+
+    def spread(buffer, size, place, device, part):
+        buffer[place] = part
+        return [
+            start(buffer.at[place], buffer.at[place], device(step))
+            for step in farthest_first(size)
+        ]
+
+    def gathered(buffer, size, copies):
+        for one in copies:
+            one.wait_recv()
+        part = buffer[0]
+        for index in range(1, size):
+            part += buffer[index]
+        return part
+
+    gain_copies = spread(gain_tp, n_tp, tp, along_tp, part)
+
     dk_send[2] = dk_acc[block(2), :].astype(jnp.bfloat16)
     dk_far_copy = start(dk_send.at[2], dk_far, along_x(3))
     dv_send[2] = dv_acc[block(2), :].astype(jnp.bfloat16)
@@ -299,29 +344,6 @@
     dv_send[1] = dv_acc[block(1), :].astype(jnp.bfloat16)
     dv_near = start(dv_send.at[1], dv_in.at[1], along_x(3))
 
-    k_gain_part = jnp.zeros((1, width), jnp.float32)
-    for head in range(heads):
-        k_gain_part += jnp.sum(
-            dk_acc[:, cols(head)] * k_unit[:, cols(head)], axis=0, keepdims=True
-        )
-    part = jnp.concatenate([q_gain_part, k_gain_part], axis=0)
-
-    def spread(buffer, size, place, device, part):
-        buffer[place] = part
-        return [
-            start(buffer.at[place], buffer.at[place], device(step)) for step in range(1, size)
-        ]
-
-    def gathered(buffer, size, copies):
-        for one in copies:
-            one.wait_recv()
-        part = buffer[0]
-        for index in range(1, size):
-            part += buffer[index]
-        return part
-
-    gain_copies = spread(gain_tp, n_tp, tp, along_tp, part)
-
     for head in range(heads):
         slot = via(head)
         dq_far_copies[head].wait_recv()
@@ -331,7 +353,7 @@
         dq_copies.append(start(dq_send.at[slot, head], dq_in.at[slot, head], device))
 
     part = gathered(gain_tp, n_tp, gain_copies)
-    gain_copies = spread(gain_z, SIDE * n_dp, z * n_dp + dp, along_z_dp, part)
+    gain_copies = spread(gain_z, ring, z_place, along_ring, part)
 
     dk_far_copy.wait_recv()
     total = dk_acc[block(1), :] + dk_far[...].astype(jnp.float32)
@@ -356,8 +378,8 @@
             grad, q_unit[0, :, cols(head)], q_inverse[:, cols(head)], q_gain_ref[...]
         ).astype(jnp.bfloat16)
 
-    part = gathered(gain_z, SIDE * n_dp, gain_copies)
-    gain_copies = spread(gain_x, SIDE, x, along_x, part)
+    part = gathered(gain_z, ring, gain_copies)
+    gain_copies = spread(gain_x, SIDE * CORES, x * CORES + core, along_x_core, part)
 
     for one in (dk_near, dv_near, dk_last, dv_last):
         one.wait_recv()
@@ -372,9 +394,24 @@
         ).astype(jnp.bfloat16)
         grad_out[2, :, cols(head)] = total.astype(jnp.bfloat16)
 
-    gain_out[...] = gathered(gain_x, SIDE, gain_copies) / length
+    gain_out[...] = gathered(gain_x, SIDE * CORES, gain_copies) / length
     for one in started:
         one.wait_send()
+
+
+def deliver(grad_in, gain_in, dq_out, dk_out, dv_out, q_gain_out, k_gain_out, sem):
+    pairs = (
+        (grad_in.at[0], dq_out.at[0]),
+        (grad_in.at[1], dk_out.at[0]),
+        (grad_in.at[2], dv_out.at[0]),
+    )
+    copies = [pltpu.make_async_copy(a, b, sem.at[i]) for i, (a, b) in enumerate(pairs)]
+    for one in copies:
+        one.start()
+    q_gain_out[...] = gain_in[0:1]
+    k_gain_out[...] = gain_in[1:2]
+    for one in copies:
+        one.wait()
 
 
 def local(q_raw, k_raw, value, d_out, q_gain, k_gain):
@@ -384,7 +421,7 @@
     n_ctx, n_tp, n_dp = (lax.axis_size(name) for name in ("ctx", "tp", "dp"))
     keys = SIDE * rows
     low, full = jnp.bfloat16, jnp.float32
-    copies = 12 + 12 + 3 * heads + 6 + SIDE * n_dp - 1 + n_tp - 1 + SIDE - 1
+    copies = 12 + 12 + 3 * heads + 6 + SIDE * n_dp // CORES - 1 + n_tp - 1 + SIDE * CORES - 1
     sizes = (n_tp, n_dp, heads, n_ctx * rows)
     block = jax.ShapeDtypeStruct((3, rows, flat), low)
     vmem = pl.BlockSpec(memory_space=pltpu.VMEM)
@@ -424,8 +461,8 @@
             pltpu.VMEM((SIDE, heads, rows, width), low),
             pltpu.VMEM((heads, rows, width), low),
             pltpu.VMEM((n_tp, 2, width), full),
-            pltpu.VMEM((SIDE * n_dp, 2, width), full),
-            pltpu.VMEM((SIDE, 2, width), full),
+            pltpu.VMEM((SIDE * n_dp // CORES, 2, width), full),
+            pltpu.VMEM((SIDE * CORES, 2, width), full),
             pltpu.SemaphoreType.DMA((6,)),
             pltpu.SemaphoreType.DMA((copies,)),
             pltpu.SemaphoreType.DMA((copies,)),
@@ -439,7 +476,17 @@
         q_gain[None],
         k_gain[None],
     )
-    return (grads[0:1], grads[1:2], grads[2:3], gains[0], gains[1])
+    one = jax.ShapeDtypeStruct((1, rows, flat), low)
+    line = jax.ShapeDtypeStruct((1, width), full)
+    hbm = pl.BlockSpec(memory_space=pl.ANY)
+    dq, dk, dv, q_part, k_part = pl.pallas_call(
+        deliver,
+        out_shape=(one, one, one, line, line),
+        in_specs=[vmem, vmem],
+        out_specs=(hbm, hbm, hbm, vmem, vmem),
+        scratch_shapes=[pltpu.SemaphoreType.DMA((3,))],
+    )(grads, gains)
+    return (dq, dk, dv, q_part[0], k_part[0])
 
 
 def solution(mesh):

time: 51.2 us -> 50 us (0.977)
  local copies, waits for them, and re-layouts: 2.76 us -> 0 us
  Pallas kernels: 47.6 us -> 49.3 us
    pallas_call x0 -> x1, Pallas kernels: none -> 2.14 us  [local(): pl.pallas_call(deliver, out_shape=(one, one, one, line, line), in_specs=[...]
    slice x1 -> x0, local copies, waits for them, and re-layouts: 1.58 us -> none  [local(): return (grads[0:1], grads[1:2], grads[2:3], gains[0], gains[1])]
    unnamed x2 -> x0, local copies, waits for them, and re-layouts: 0.66 us -> none
    squeeze x1 -> x0, local copies, waits for them, and re-layouts: 0.52 us -> none  [local(): return (grads[0:1], grads[1:2], grads[2:3], gains[0], gains[1])]
where the time goes in v4:
time: 50 us; the launch traced here: 49.9 us
  Pallas kernels  49.3 us (99%)
  between operations  0.64 us (1%)
    pallas_call x1, Pallas kernels, local(): pl.pallas_call(functools.partial(kernel, sizes), out_shape=(block, jax.Sh...  47.1 us
    pallas_call x1, Pallas kernels, local(): pl.pallas_call(deliver, out_shape=(one, one, one, line, line), in_specs=[...  2.14 us

profile of v4, /device:TPU:1, one launch (start us, length us, event | category | flops | bytes accessed | tf_op | source)
XLA Modules:
  0.0 49.9 jit_solution(10489803859720823981)
XLA Ops:
  0.6 47.1 %shard_map.101 = (bf16[3,128,256]{2,1,0:T(8,128)(2,1)}, f32[2,128]{1,0:T(2,128)}) custom-call(bf16[128,256]{1,0:T(8,128)(2,1)} %bitcast.8, bf16[128,256]{1,0:T(8,128)(2,1)} %bitcast.9, bf16[128,256]{1,0:T(8,128)(2,1)} %bitcast.10, bf16[128,256]{1,0:T(8,128)(2,1)} %bitcast.11, f32[1,128]{1,0:T(1,128)} %bitcast.12, f32[1,128]{1,0:T(1,128)} %bitcast.13), custom_call_target="tpu_custom_call" | custom-call | tf_op jit(solution)/shard_map/pallas_call | solution.py:428
  47.7 2.1 %shard_map.102 = (bf16[1,128,256]{2,1,0:T(8,128)(2,1)}, bf16[1,128,256]{2,1,0:T(8,128)(2,1)}, bf16[1,128,256]{2,1,0:T(8,128)(2,1)}, f32[1,128]{1,0:T(1,128)}, f32[1,128]{1,0:T(1,128)}) custom-call(bf16[3,128,256]{2,1,0:T(8,128)(2,1)} %get-tuple-element.12.grad_in, f32[2,128]{1,0:T(2,128)} %get-tuple-element.13.gain_in), custom_call_target="tpu_custom_call" | custom-call | tf_op jit(solution)/shard_map/pallas_call | solution.py:482

commit v5 on v4

--- a/solution.py
+++ b/solution.py
@@ -54,7 +54,6 @@
     dq_far,
     gain_tp,
     gain_z,
-    gain_x,
     load_sem,
     send_sem,
     recv_sem,
@@ -81,34 +80,35 @@
     core = lax.rem(dp, CORES)
     z_place = z * chips + dp // CORES
 
-    def along_ring(step):
-        place = lax.rem(z_place + step, ring)
+    def along_ring_x(step):
+        place = lax.rem(z_place + step // SIDE, ring)
         return {
-            "ctx": place // chips * SIDE + x,
+            "ctx": place // chips * SIDE + lax.rem(x + step % SIDE, SIDE),
             "tp": tp,
             "dp": lax.rem(place, chips) * CORES + core,
         }
 
-    def along_x_core(step):
+    def along_tp_core(step):
         return {
-            "ctx": z * SIDE + lax.rem(x + step // CORES, SIDE),
-            "tp": tp,
+            "ctx": ctx,
+            "tp": lax.rem(tp + step // CORES, n_tp),
             "dp": dp - core + lax.rem(core + step % CORES, CORES),
         }
 
-    def along_tp(step):
-        return {"ctx": ctx, "tp": lax.rem(tp + step, n_tp), "dp": dp}
+    def farthest_first(outer, inner):
+        def hops(step):
+            far, near = step // inner, step % inner
+            return min(far, outer - far) + min(near, inner - near)
+
+        return sorted(range(1, outer * inner), key=lambda step: -hops(step))
+
+    ring_steps = farthest_first(ring, SIDE)
+    tp_steps = farthest_first(n_tp, CORES)
 
     barrier = pltpu.get_barrier_semaphore()
-
-    def farthest_first(size):
-        return sorted(range(1, size), key=lambda step: -min(step, size - step))
-
-    partners = (
-        [along_ring(step) for step in farthest_first(ring)]
-        + [along_tp(step) for step in farthest_first(n_tp)]
-        + [along_x_core(step) for step in farthest_first(SIDE * CORES)]
-    )
+    partners = [along_ring_x(step) for step in ring_steps] + [
+        along_tp_core(step) for step in tp_steps
+    ]
     for partner in partners:
         pl.semaphore_signal(barrier, inc=1, device_id=partner, device_id_type=MESH)
 
@@ -318,22 +318,19 @@
         )
     part = jnp.concatenate([q_gain_part, k_gain_part], axis=0)
 
-    def spread(buffer, size, place, device, part):
+    def spread(buffer, steps, place, device, part):
         buffer[place] = part
-        return [
-            start(buffer.at[place], buffer.at[place], device(step))
-            for step in farthest_first(size)
-        ]
-
-    def gathered(buffer, size, copies):
+        return [start(buffer.at[place], buffer.at[place], device(step)) for step in steps]
+
+    def gathered(buffer, copies):
         for one in copies:
             one.wait_recv()
         part = buffer[0]
-        for index in range(1, size):
+        for index in range(1, len(copies) + 1):
             part += buffer[index]
         return part
 
-    gain_copies = spread(gain_tp, n_tp, tp, along_tp, part)
+    gain_copies = spread(gain_tp, tp_steps, tp * CORES + core, along_tp_core, part)
 
     dk_send[2] = dk_acc[block(2), :].astype(jnp.bfloat16)
     dk_far_copy = start(dk_send.at[2], dk_far, along_x(3))
@@ -352,9 +349,6 @@
         device = along_z(SIDE - slot)
         dq_copies.append(start(dq_send.at[slot, head], dq_in.at[slot, head], device))
 
-    part = gathered(gain_tp, n_tp, gain_copies)
-    gain_copies = spread(gain_z, ring, z_place, along_ring, part)
-
     dk_far_copy.wait_recv()
     total = dk_acc[block(1), :] + dk_far[...].astype(jnp.float32)
     dk_send[1] = total.astype(jnp.bfloat16)
@@ -363,6 +357,9 @@
     total = dv_acc[block(3), :] + dv_far[...].astype(jnp.float32)
     dv_send[3] = total.astype(jnp.bfloat16)
     dv_last = start(dv_send.at[3], dv_in.at[3], along_x(1))
+
+    part = gathered(gain_tp, gain_copies)
+    gain_copies = spread(gain_z, ring_steps, z_place * SIDE + x, along_ring_x, part)
 
     def restore(grad, unit, inverse, gain):
         scaled = grad * gain
@@ -377,9 +374,6 @@
         grad_out[0, :, cols(head)] = restore(
             grad, q_unit[0, :, cols(head)], q_inverse[:, cols(head)], q_gain_ref[...]
         ).astype(jnp.bfloat16)
-
-    part = gathered(gain_z, ring, gain_copies)
-    gain_copies = spread(gain_x, SIDE * CORES, x * CORES + core, along_x_core, part)
 
     for one in (dk_near, dv_near, dk_last, dv_last):
         one.wait_recv()
@@ -394,7 +388,7 @@
         ).astype(jnp.bfloat16)
         grad_out[2, :, cols(head)] = total.astype(jnp.bfloat16)
 
-    gain_out[...] = gathered(gain_x, SIDE * CORES, gain_copies) / length
+    gain_out[...] = gathered(gain_z, gain_copies) / length
     for one in started:
         one.wait_send()
 
@@ -421,7 +415,7 @@
     n_ctx, n_tp, n_dp = (lax.axis_size(name) for name in ("ctx", "tp", "dp"))
     keys = SIDE * rows
     low, full = jnp.bfloat16, jnp.float32
-    copies = 12 + 12 + 3 * heads + 6 + SIDE * n_dp // CORES - 1 + n_tp - 1 + SIDE * CORES - 1
+    copies = 12 + 12 + 3 * heads + 6 + SIDE * SIDE * n_dp // CORES - 1 + n_tp * CORES - 1
     sizes = (n_tp, n_dp, heads, n_ctx * rows)
     block = jax.ShapeDtypeStruct((3, rows, flat), low)
     vmem = pl.BlockSpec(memory_space=pltpu.VMEM)
@@ -460,9 +454,8 @@
             pltpu.VMEM((SIDE, heads, rows, width), low),
             pltpu.VMEM((SIDE, heads, rows, width), low),
             pltpu.VMEM((heads, rows, width), low),
-            pltpu.VMEM((n_tp, 2, width), full),
-            pltpu.VMEM((SIDE * n_dp // CORES, 2, width), full),
-            pltpu.VMEM((SIDE * CORES, 2, width), full),
+            pltpu.VMEM((n_tp * CORES, 2, width), full),
+            pltpu.VMEM((SIDE * SIDE * n_dp // CORES, 2, width), full),
             pltpu.SemaphoreType.DMA((6,)),
             pltpu.SemaphoreType.DMA((copies,)),
             pltpu.SemaphoreType.DMA((copies,)),

time: 50 us -> 49 us (0.980)
  Pallas kernels: 49.3 us -> 48.3 us
    pallas_call x1, Pallas kernels: 47.1 us -> 46.1 us  [local(): pl.pallas_call(functools.partial(kernel, sizes), out_shape=(block, jax.Sh...]
where the time goes in v5:
time: 49 us; the launch traced here: 48.9 us
  Pallas kernels  48.3 us (99%)
  between operations  0.64 us (1%)
    pallas_call x1, Pallas kernels, local(): pl.pallas_call(functools.partial(kernel, sizes), out_shape=(block, jax.Sh...  46.1 us
    pallas_call x1, Pallas kernels, local(): pl.pallas_call(deliver, out_shape=(one, one, one, line, line), in_specs=[...  2.14 us

profile of v5, /device:TPU:1, one launch (start us, length us, event | category | flops | bytes accessed | tf_op | source)
XLA Modules:
  0.0 48.9 jit_solution(5973229928204234715)
XLA Ops:
  0.6 46.1 %shard_map.101 = (bf16[3,128,256]{2,1,0:T(8,128)(2,1)}, f32[2,128]{1,0:T(2,128)}) custom-call(bf16[128,256]{1,0:T(8,128)(2,1)} %bitcast.8, bf16[128,256]{1,0:T(8,128)(2,1)} %bitcast.9, bf16[128,256]{1,0:T(8,128)(2,1)} %bitcast.10, bf16[128,256]{1,0:T(8,128)(2,1)} %bitcast.11, f32[1,128]{1,0:T(1,128)} %bitcast.12, f32[1,128]{1,0:T(1,128)} %bitcast.13), custom_call_target="tpu_custom_call" | custom-call | tf_op jit(solution)/shard_map/pallas_call | solution.py:422
  46.7 2.1 %shard_map.102 = (bf16[1,128,256]{2,1,0:T(8,128)(2,1)}, bf16[1,128,256]{2,1,0:T(8,128)(2,1)}, bf16[1,128,256]{2,1,0:T(8,128)(2,1)}, f32[1,128]{1,0:T(1,128)}, f32[1,128]{1,0:T(1,128)}) custom-call(bf16[3,128,256]{2,1,0:T(8,128)(2,1)} %get-tuple-element.12.grad_in, f32[2,128]{1,0:T(2,128)} %get-tuple-element.13.gain_in), custom_call_target="tpu_custom_call" | custom-call | tf_op jit(solution)/shard_map/pallas_call | solution.py:475

commit v6 on v5

--- a/solution.py
+++ b/solution.py
@@ -150,23 +150,23 @@
 
     pl.semaphore_wait(barrier, len(partners))
 
-    q_up = copy(q_hbm, q_raw.at[1], along_z(1))
+    halves = [pl.ds(0, rows // 2), pl.ds(rows // 2, rows // 2)]
+    q_up = [copy(q_hbm.at[half], q_raw.at[1, half], along_z(1)) for half in halves]
     q_down = copy(q_hbm, q_raw.at[3], along_z(3))
     o_up = copy(o_hbm, o_all.at[1], along_z(1))
-    o_down = copy(o_hbm, o_all.at[3], along_z(3))
+    o_down = [copy(o_hbm.at[half], o_all.at[3, half], along_z(3)) for half in halves]
     k_up = copy(k_hbm, k_raw.at[1], along_x(1))
     k_down = copy(k_hbm, k_raw.at[3], along_x(3))
     v_up = copy(v_hbm, v_all.at[1], along_x(1))
     v_down = copy(v_hbm, v_all.at[3], along_x(3))
-    for one in (q_up, o_down, k_up, v_down, o_up, q_down, v_up, k_down):
+    first = (q_up[0], o_down[0], q_up[1], o_down[1])
+    for one in first + (k_up, v_down, o_up, q_down, v_up, k_down):
         one.start()
-    q_far = copy(q_raw.at[1], q_raw.at[2], along_z(1))
-    o_far = copy(o_all.at[3], o_all.at[2], along_z(3))
+    q_far = [copy(q_raw.at[1, half], q_raw.at[2, half], along_z(1)) for half in halves]
+    o_far = [copy(o_all.at[3, half], o_all.at[2, half], along_z(3)) for half in halves]
     k_far = copy(k_raw.at[1], k_raw.at[2], along_x(1))
     v_far = copy(v_all.at[3], v_all.at[2], along_x(3))
 
-    dk_acc[...] = jnp.zeros_like(dk_acc)
-    dv_acc[...] = jnp.zeros_like(dv_acc)
     stat_own[...] = jnp.zeros_like(stat_own)
     for one in loads:
         one.wait()
@@ -205,10 +205,11 @@
     k_down.wait_recv()
     norm_k(3)
     v_up.wait_recv()
-    q_up.wait_recv()
-    q_far.start()
-    o_down.wait_recv()
-    o_far.start()
+    for half in range(2):
+        q_up[half].wait_recv()
+        q_far[half].start()
+        o_down[half].wait_recv()
+        o_far[half].start()
     k_far.wait_recv()
     norm_k(2)
     v_far.wait_recv()
@@ -231,7 +232,7 @@
                 v_all[:, :, cols(head)].reshape(keys, width), o_all[slot, :, cols(head)]
             )
             expo[slot, head] = weights
-            dprob[slot, head] = slopes
+            dprob[slot, head] = slopes * scale
             stat_own[slot, 3 * head : 3 * head + 1] = top
             stat_own[slot, 3 * head + 1 : 3 * head + 2] = jnp.sum(weights, axis=0, keepdims=True)
             stat_own[slot, 3 * head + 2 : 3 * head + 3] = jnp.sum(
@@ -250,9 +251,11 @@
     q_down.wait_recv()
     norm_q(3)
     first_pass(3)
-    q_far.wait_recv()
+    for one in q_far:
+        one.wait_recv()
     norm_q(2)
-    o_far.wait_recv()
+    for one in o_far:
+        one.wait_recv()
     first_pass(2)
 
     def second_pass(slot):
@@ -272,17 +275,23 @@
             total = sum(one * factor for one, factor in zip(totals, factors))
             delta = sum(one * factor for one, factor in zip(weighted, factors)) / total
             prob = expo[slot, head] * (factors[0] / total)
-            dscore = (prob * (dprob[slot, head] - delta) * scale).astype(jnp.bfloat16)
+            dscore = (prob * (dprob[slot, head] - delta * scale)).astype(jnp.bfloat16)
             prob_low = prob.astype(jnp.bfloat16)
             dq = jnp.dot(k_turned[head], dscore, preferred_element_type=jnp.float32).T
             part += jnp.sum(dq * q_unit[slot, :, cols(head)], axis=0, keepdims=True)
             dq_full[slot, head] = dq
-            dk_acc[:, cols(head)] += jnp.dot(
+            dk = jnp.dot(
                 dscore, q_normed[slot, :, cols(head)], preferred_element_type=jnp.float32
             )
-            dv_acc[:, cols(head)] += jnp.dot(
+            dv = jnp.dot(
                 prob_low, o_all[slot, :, cols(head)], preferred_element_type=jnp.float32
             )
+            if slot == 2:
+                dk_acc[:, cols(head)] = dk
+                dv_acc[:, cols(head)] = dv
+            else:
+                dk_acc[:, cols(head)] += dk
+                dv_acc[:, cols(head)] += dv
         return part
 
     def via(head):
@@ -415,7 +424,7 @@
     n_ctx, n_tp, n_dp = (lax.axis_size(name) for name in ("ctx", "tp", "dp"))
     keys = SIDE * rows
     low, full = jnp.bfloat16, jnp.float32
-    copies = 12 + 12 + 3 * heads + 6 + SIDE * SIDE * n_dp // CORES - 1 + n_tp * CORES - 1
+    copies = 16 + 12 + 3 * heads + 6 + SIDE * SIDE * n_dp // CORES - 1 + n_tp * CORES - 1
     sizes = (n_tp, n_dp, heads, n_ctx * rows)
     block = jax.ShapeDtypeStruct((3, rows, flat), low)
     vmem = pl.BlockSpec(memory_space=pltpu.VMEM)

time: 49 us -> 48.6 us (level)
  Pallas kernels: 48.3 us -> 47.8 us
where the time goes in v6:
time: 48.6 us; the launch traced here: 48.5 us
  Pallas kernels  47.8 us (98%)
  between operations  0.64 us (1%)
    pallas_call x1, Pallas kernels, local(): pl.pallas_call(functools.partial(kernel, sizes), out_shape=(block, jax.Sh...  45.7 us
    pallas_call x1, Pallas kernels, local(): pl.pallas_call(deliver, out_shape=(one, one, one, line, line), in_specs=[...  2.14 us

profile of v6, /device:TPU:1, one launch (start us, length us, event | category | flops | bytes accessed | tf_op | source)
XLA Modules:
  0.0 48.5 jit_solution(17853076184368926225)
XLA Ops:
  0.6 45.7 %shard_map.101 = (bf16[3,128,256]{2,1,0:T(8,128)(2,1)}, f32[2,128]{1,0:T(2,128)}) custom-call(bf16[128,256]{1,0:T(8,128)(2,1)} %bitcast.8, bf16[128,256]{1,0:T(8,128)(2,1)} %bitcast.9, bf16[128,256]{1,0:T(8,128)(2,1)} %bitcast.10, bf16[128,256]{1,0:T(8,128)(2,1)} %bitcast.11, f32[1,128]{1,0:T(1,128)} %bitcast.12, f32[1,128]{1,0:T(1,128)} %bitcast.13), custom_call_target="tpu_custom_call" | custom-call | tf_op jit(solution)/shard_map/pallas_call | solution.py:431
  46.3 2.1 %shard_map.102 = (bf16[1,128,256]{2,1,0:T(8,128)(2,1)}, bf16[1,128,256]{2,1,0:T(8,128)(2,1)}, bf16[1,128,256]{2,1,0:T(8,128)(2,1)}, f32[1,128]{1,0:T(1,128)}, f32[1,128]{1,0:T(1,128)}) custom-call(bf16[3,128,256]{2,1,0:T(8,128)(2,1)} %get-tuple-element.12.grad_in, f32[2,128]{1,0:T(2,128)} %get-tuple-element.13.gain_in), custom_call_target="tpu_custom_call" | custom-call | tf_op jit(solution)/shard_map/pallas_call | solution.py:484
